TPU v7x, 32 devices: a whole 2x2x4 slice. The times are simulated.
32 devices in a mesh: dp: 8 (over z, x), tensor: 4 (over y, core).
Axes of the slice: x: 2, y: 2, z: 4, core: 2. Of those that a mesh axis runs over, the one named last changes fastest.
Arguments:
- stream_in: bfloat16 [8, 1024, 2048], P('dp', 'tensor'), may hold values from -6 to 6
- segments: int32 [8, 1024], P('dp'), may hold values from 0 to 2, never falling along the last dimension, each value on 1 to 800 neighbouring positions
- first_gain: float32 [2048], replicated, may hold values from 0.5 to 1.5
- gelu_gate_weight: bfloat16 [2048, 2560], P(None, 'tensor'), may hold values from -0.125 to 0.125
- recurrent_branch_weight: bfloat16 [2048, 2560], P(None, 'tensor'), may hold values from -0.125 to 0.125
- conv_kernel: float32 [4, 2560], P(None, 'tensor'), may hold values from -3 to 3
- conv_bias: float32 [2560], P('tensor'), may hold values from -3 to 3
- recur_weight: bfloat16 [16, 160, 160], P('tensor'), may hold values from -0.5 to 0.5
- recur_bias: float32 [2560], P('tensor'), may hold values from -4 to 4
- inlet_weight: bfloat16 [16, 160, 160], P('tensor'), may hold values from -0.5 to 0.5
- inlet_bias: float32 [2560], P('tensor'), may hold values from -3 to 3
- decay_param: float32 [2560], P('tensor'), may hold values from 5 to 9
- recurrent_output_weight: bfloat16 [2560, 2048], P('tensor'), may hold values from -0.25 to 0.25
- second_gain: float32 [2048], replicated, may hold values from 0.5 to 1.5
- gate_projection_weight: bfloat16 [2048, 6144], P(None, 'tensor'), may hold values from -0.125 to 0.125
- up_projection_weight: bfloat16 [2048, 6144], P(None, 'tensor'), may hold values from -0.125 to 0.125
- down_projection_weight: bfloat16 [6144, 2048], P('tensor'), may hold values from -0.15625 to 0.15625
- cotangent: bfloat16 [8, 1024, 2048], P('dp', 'tensor'), may hold values from -6 to 6
Outputs:
- stream_out: float32 [8, 1024, 2048], P('dp', 'tensor')
- stream_grad: float32 [8, 1024, 2048], P('dp', 'tensor')
- first_gain_grad: float32 [2048], replicated
- gated_weight_grad: float32 [2048, 2560], P('dp', 'tensor')
- branch_weight_grad: float32 [2048, 2560], P('dp', 'tensor')
- conv_kernel_grad: float32 [4, 2560], P(None, 'tensor')
- conv_bias_grad: float32 [2560], P('tensor')
- recur_weight_grad: float32 [16, 160, 160], P('tensor')
- recur_bias_grad: float32 [2560], P('tensor')
- inlet_weight_grad: float32 [16, 160, 160], P('tensor')
- inlet_bias_grad: float32 [2560], P('tensor')
- decay_param_grad: float32 [2560], P('tensor')
- output_weight_grad: float32 [2560, 2048], P('tensor', 'dp')
- second_gain_grad: float32 [2048], replicated
- hidden_gate_grad: float32 [2048, 6144], P('dp', 'tensor')
- hidden_up_grad: float32 [2048, 6144], P('dp', 'tensor')
- hidden_down_grad: float32 [6144, 2048], P('tensor', 'dp')
Inputs may be any that keep to these rules, and one draw needn't show every extreme that they name: `segments`: segment numbers never fall along a sequence; a document starts at position 0 and wherever the number changes, and no document is longer than 800 tokens.
All inputs are finite; a program needn't handle non-finite values.
Results may differ from a plain program's by a relative error of at most 0.0085.
Values may be sent and summed in bfloat16 or wider, within the bound.
A program may use at most 256 MiB of HBM per device.

v0:
```python
import functools

import jax
import jax.numpy as jnp
from jax import lax
from jax.experimental import pallas as pl
from jax.experimental.pallas import tpu as pltpu
from jax.sharding import PartitionSpec as P

epsilon = 1e-06
decay_scale = 8.0
LANES = 128
GELU_C = 0.7978845608028654
GELU_K = 0.044715
F32 = jnp.float32
BF16 = jnp.bfloat16
VMEM_BYTES = 60 * 1024 * 1024


def minus_expm1(y, exp_y):
    s = 1.0 + y * (1.0 / 9.0)
    for d in range(8, 1, -1):
        s = 1.0 + (y * (1.0 / d)) * s
    return jnp.where(y > -0.5, -y * s, 1.0 - exp_y)


def gelu_parts(v):
    v2 = v * v
    t = jnp.tanh(GELU_C * v * (1.0 + GELU_K * v2))
    half = 0.5 * (1.0 + t)
    slope = half + 0.5 * v * (1.0 - t * t) * (GELU_C * (1.0 + 3.0 * GELU_K * v2))
    return v * half, slope


def lane_tiles(width):
    return [slice(j * LANES, (j + 1) * LANES) for j in range(width // LANES)]


def fold_rows(v):
    return jnp.sum(v.reshape(v.shape[0] // 8, 8, v.shape[1]), axis=0)


def gates_pre(rows, step, conv_ref, w_ref, pre_s):
    @pl.loop(0, rows // step)
    def _(i):
        r = pl.ds(pl.multiple_of(i * step, step), step)
        pre_s[r, :] = jnp.dot(conv_ref[r, :], w_ref[...], preferred_element_type=F32)


def mixer_forward_kernel(branch_ref, gated_ref, mask_ref, vec_ref, w_ref, conv_ref, states_ref, product_ref, pre_s, a_s, b_s):
    rows, width = branch_ref.shape
    seg = rows // 8
    tiles = lane_tiles(width)

    @pl.loop(0, 8)
    def _(s):
        t0 = pl.multiple_of(s * seg, seg)
        before = pl.multiple_of(jnp.maximum(t0 - 8, 0), 8)
        same = [mask_ref[pl.ds(t0, seg), k : k + 1] for k in range(3)]
        for cols in tiles:
            b = branch_ref[pl.ds(t0, seg), cols]
            ext = jnp.concatenate([branch_ref[pl.ds(before, 8), cols], b], axis=0)
            out = vec_ref[4:5, cols] + vec_ref[0:1, cols] * b
            for k in range(1, 4):
                out = out + vec_ref[k : k + 1, cols] * pltpu.roll(ext, k, 0)[8:] * same[k - 1]
            conv_ref[pl.ds(t0, seg), cols] = out.astype(BF16)

    gates_pre(rows, 256, conv_ref, w_ref, pre_s)

    @pl.loop(0, 8)
    def _(s):
        t0 = pl.multiple_of(s * seg, seg)
        c = mask_ref[pl.ds(t0, seg), 0:1]
        for j, cols in enumerate(tiles):
            cols_i = slice(width + j * LANES, width + (j + 1) * LANES)
            r = jax.nn.sigmoid(pre_s[pl.ds(t0, seg), cols] + vec_ref[5:6, cols])
            i = jax.nn.sigmoid(pre_s[pl.ds(t0, seg), cols_i] + vec_ref[6:7, cols])
            log_a = (-decay_scale * vec_ref[7:8, cols]) * r
            a = jnp.exp(log_a)
            n = jnp.sqrt(minus_expm1(2.0 * log_a, a * a))
            mult = (1.0 - c) + c * n
            a_s[j, pl.ds(t0, seg), :] = a * c
            b_s[j, pl.ds(t0, seg), :] = mult * i * conv_ref[pl.ds(t0, seg), cols].astype(F32)

    row = lax.broadcasted_iota(jnp.int32, (8, LANES), 0)

    def scan_step(i, carry):
        at = pl.ds(pl.multiple_of(i * 8, 8), 8)
        out = []
        for j, cols in enumerate(tiles):
            a, b = a_s[j, at, :], b_s[j, at, :]
            for s in (1, 2, 4):
                b = b + a * jnp.where(row >= s, pltpu.roll(b, s, 0), 0.0)
                a = a * jnp.where(row >= s, pltpu.roll(a, s, 0), 1.0)
            b = b + a * carry[j]
            states_ref[at, cols] = b
            out.append(jnp.broadcast_to(b[7:8, :], (8, LANES)))
        return tuple(out)

    lax.fori_loop(0, rows // 8, scan_step, tuple(jnp.zeros((8, LANES), F32) for _ in tiles), unroll=2)

    @pl.loop(0, 8)
    def _(s):
        at = pl.ds(pl.multiple_of(s * seg, seg), seg)
        for cols in tiles:
            act, _ = gelu_parts(gated_ref[at, cols])
            product_ref[at, cols] = (states_ref[at, cols] * act).astype(BF16)


class MixerBackward:
    def __init__(self, masks, vecs, w_cat, states, branch, conv, dgated, dri, dbranch, sums, pre_s, a_s, n_s, ac_s, e_s):
        self.masks, self.vecs, self.w_cat, self.states, self.branch, self.conv = masks, vecs, w_cat, states, branch, conv
        self.dgated, self.dri, self.dbranch, self.sums = dgated, dri, dbranch, sums
        self.pre_s, self.a_s, self.n_s, self.ac_s, self.e_s = pre_s, a_s, n_s, ac_s, e_s
        self.rows, self.width = states.shape
        self.seg = self.rows // 8
        self.tiles = lane_tiles(self.width)

    @staticmethod
    def scratch(rows, width):
        lanes = width // LANES
        return [
            pltpu.VMEM((rows, 2 * width), F32),
            pltpu.VMEM((rows, width), F32),
            pltpu.VMEM((rows + 8, width), F32),
            pltpu.VMEM((lanes, rows, LANES), F32),
            pltpu.VMEM((lanes, rows, LANES), F32),
        ]

    def gates(self):
        self.sums[...] = jnp.zeros_like(self.sums)
        gates_pre(self.rows, 256, self.conv, self.w_cat, self.pre_s)

    def factors(self, gated):
        @pl.loop(0, 8)
        def _(s):
            t0 = pl.multiple_of(s * self.seg, self.seg)
            at = pl.ds(t0, self.seg)
            c = self.masks[at, 0:1]
            for j, cols in enumerate(self.tiles):
                cols_i = slice(self.width + j * LANES, self.width + (j + 1) * LANES)
                r = jax.nn.sigmoid(self.pre_s[at, cols] + self.vecs[5:6, cols])
                self.pre_s[at, cols] = r
                self.pre_s[at, cols_i] = jax.nn.sigmoid(self.pre_s[at, cols_i] + self.vecs[6:7, cols])
                log_a = (-decay_scale * self.vecs[7:8, cols]) * r
                a = jnp.exp(log_a)
                d = self.a_s[at, cols]
                self.a_s[at, cols] = a
                self.n_s[at, cols] = jnp.sqrt(minus_expm1(2.0 * log_a, a * a))
                self.ac_s[j, at, :] = a * c
                act, slope = gelu_parts(gated[at, cols])
                self.e_s[j, at, :] = d * act
                self.dgated[at, cols] = (d * self.states[at, cols] * slope).astype(BF16)

    def scan(self):
        row = lax.broadcasted_iota(jnp.int32, (8, LANES), 0)

        def step(q, carry):
            at = pl.ds(pl.multiple_of((self.rows // 8 - 1 - q) * 8, 8), 8)
            out = []
            for j in range(len(self.tiles)):
                e, later = carry[j]
                now = self.ac_s[j, at, :]
                a = jnp.where(row == 7, later, pltpu.roll(now, 7, 0))
                b = self.e_s[j, at, :]
                for s in (1, 2, 4):
                    b = b + a * jnp.where(row < 8 - s, pltpu.roll(b, 8 - s, 0), 0.0)
                    a = a * jnp.where(row < 8 - s, pltpu.roll(a, 8 - s, 0), 1.0)
                b = b + a * e
                self.e_s[j, at, :] = b
                out.append((jnp.broadcast_to(b[0:1, :], (8, LANES)), jnp.broadcast_to(now[0:1, :], (8, LANES))))
            return tuple(out)

        none = jnp.zeros((8, LANES), F32)
        lax.fori_loop(0, self.rows // 8, step, tuple((none, none) for _ in self.tiles), unroll=2)

    def gate_gradients(self):
        seg, width = self.seg, self.width

        @pl.loop(0, 8)
        def _(s):
            t0 = pl.multiple_of(s * seg, seg)
            at = pl.ds(t0, seg)
            before = pl.multiple_of(jnp.maximum(t0 - 8, 0), 8)
            c = self.masks[at, 0:1]
            for j, cols in enumerate(self.tiles):
                cols_i = slice(width + j * LANES, width + (j + 1) * LANES)
                e = self.e_s[j, at, :]
                ext = jnp.concatenate([self.states[pl.ds(before, 8), cols], self.states[at, cols]], axis=0)
                earlier = pltpu.roll(ext, 1, 0)[8:]
                r, i, a, n = self.pre_s[at, cols], self.pre_s[at, cols_i], self.a_s[at, cols], self.n_s[at, cols]
                cv = self.conv[at, cols].astype(F32)
                ec = e * c
                d_log = a * (ec * earlier) - ec * i * cv * (a * a / n)
                rr = d_log * r
                dr = ((-decay_scale * self.vecs[7:8, cols]) * rr * (1.0 - r)).astype(BF16)
                em = e * ((1.0 - c) + c * n) * i
                di = (em * cv * (1.0 - i)).astype(BF16)
                self.dri[at, cols] = dr
                self.dri[at, cols_i] = di
                self.n_s[at, cols] = em
                self.sums[5, :, cols] += fold_rows(dr.astype(F32))
                self.sums[6, :, cols] += fold_rows(di.astype(F32))
                self.sums[7, :, cols] += fold_rows(rr)

        @pl.loop(0, self.rows // 256)
        def _(i):
            at = pl.ds(pl.multiple_of(i * 256, 256), 256)
            self.n_s[at, :] += dot_nt(self.dri[at, :], self.w_cat[...])

        self.n_s[self.rows : self.rows + 8, :] = jnp.zeros((8, width), F32)

    def convolution(self):
        @pl.loop(0, 8)
        def _(s):
            t0 = pl.multiple_of(s * self.seg, self.seg)
            at, ext = pl.ds(t0, self.seg), pl.ds(t0, self.seg + 8)
            same = [self.masks[ext, k : k + 1] for k in range(3)]
            for cols in self.tiles:
                d = self.n_s[ext, cols]
                b = self.branch[at, cols]
                self.sums[4, :, cols] += fold_rows(d[: self.seg])
                self.sums[0, :, cols] += fold_rows(d[: self.seg] * b)
                total = self.vecs[0:1, cols] * d[: self.seg]
                for k in range(1, 4):
                    moved = pltpu.roll(d * same[k - 1], self.seg + 8 - k, 0)[: self.seg]
                    total = total + self.vecs[k : k + 1, cols] * moved
                    self.sums[k, :, cols] += fold_rows(moved * b)
                self.dbranch[at, cols] = total.astype(BF16)


def dot_nt(left, right):
    return lax.dot_general(left, right, (((1,), (1,)), ((), ())), preferred_element_type=F32)


class Stage:
    def __init__(self, stride, size, later):
        self.stride, self.size, self.later = stride, size, later
        self.blocks = 1
        for s in later:
            self.blocks *= s.size
        self.digit = lax.rem(lax.axis_index("dp") // stride, size)

    def offset(self, position):
        total = 0
        for s in reversed(self.later):
            total = total + lax.rem(position, s.size) * s.stride
            position = position // s.size
        return total


def digit_sizes(n):
    if n == 8:
        return [2, 4]
    sizes = []
    while n > 1:
        m = 4 if n % 4 == 0 else 2 if n % 2 == 0 else n
        sizes.append(m)
        n //= m
    return sizes


def make_stages(n, last_first):
    digits, stride = [], 1
    for m in digit_sizes(n):
        digits.append((stride, m))
        stride *= m
    if last_first:
        digits = digits[1:] + digits[:1]
    stages = []
    for stride, m in reversed(digits):
        stages.insert(0, Stage(stride, m, list(stages)))
    return stages


class Item:
    def __init__(self, stages, left, right, width, ready, refs, resident=None):
        self.stages, self.left, self.right, self.width, self.ready = stages, left, right, width, ready
        self.resident = resident
        self.columns = right.shape[1]
        self.out, self.recv, self.send, self.send_sem, self.recv_sem = refs

    def message(self, t, back, k, slot, rows=None):
        stage = self.stages[t]
        rows = pl.ds(0, stage.blocks * self.width) if rows is None else rows
        step = jnp.where(back, -stage.stride, stage.stride)
        return pltpu.make_async_remote_copy(
            src_ref=self.send[t].at[slot, rows],
            dst_ref=self.recv[t].at[back, k - 1, rows],
            send_sem=self.send_sem[t].at[slot],
            recv_sem=self.recv_sem[t].at[back, k - 1],
            device_id={"dp": lax.axis_index("dp") + step},
            device_id_type=pl.DeviceIdType.MESH,
        )


class Engine:
    def __init__(self, left_s, got_s, total_s, sem, out_s=None, out_sem=None):
        self.left_s, self.got_s, self.total_s, self.sem = left_s, got_s, total_s, sem
        self.out_s, self.out_sem, self.finished = out_s, out_sem, None

    def fetch(self, item, block, slot):
        if len(item.left.shape) == 3:
            source = item.left.at[block]
        else:
            size = max(item.width, LANES)
            source = item.left.at[:, pl.ds(pl.multiple_of(block // (size // item.width) * size, size), size)]
        return pltpu.make_async_copy(source, self.left_s.at[slot], self.sem.at[slot])

    def columns(self, item, block, slot):
        held = self.left_s[slot]
        if held.shape[1] == item.width:
            return held
        pieces = [held[:, i * item.width : (i + 1) * item.width] for i in range(held.shape[1] // item.width)]
        value = pieces[0]
        for i, piece in enumerate(pieces[1:], 1):
            value = jnp.where(lax.rem(block, len(pieces)) == i, piece, value)
        return value

    def products(self, item, count, block_of, store, done):
        tile = item.columns // 2 if item.columns > 1024 else item.columns

        def compute(p, left):
            if tile == item.columns:
                store(p, pl.ds(0, tile), dot_tn(left(), item.right[...]))
            else:

                @pl.loop(0, item.columns // tile)
                def _(c):
                    cols = pl.ds(pl.multiple_of(c * tile, tile), tile)
                    store(p, cols, dot_tn(left(), item.right[:, cols]))

            done(p)

        if item.resident is not None:

            @pl.loop(0, count)
            def _(p):
                cols = pl.ds(pl.multiple_of(block_of(p) * item.width, item.width), item.width)
                compute(p, lambda: item.resident[:, cols])

            return
        self.fetch(item, block_of(0), 0).start()

        @pl.loop(0, count)
        def _(p):
            slot = lax.rem(p, 2)
            if count > 1:

                @pl.when(p + 1 < count)
                def _():
                    self.fetch(item, block_of(p + 1), 1 - slot).start()

            self.fetch(item, block_of(p), slot).wait()
            compute(p, lambda: self.columns(item, block_of(p), slot))

    def got_copy(self, item, i, source):
        return pltpu.make_async_copy(source, self.got_s.at[i, :, pl.ds(0, item.columns)], self.sem.at[2 + i])

    def start_gots(self, item, first, gots):
        for i, (condition, source) in enumerate(gots):

            @pl.when(condition)
            def _(i=i, source=source):
                self.got_copy(item, first + i, source).start()

    def add_gots(self, item, gots, put):
        for i, (condition, source) in enumerate(gots):

            @pl.when(condition)
            def _(i=i, source=source):
                self.got_copy(item, i, source).wait()

        @pl.loop(0, item.width // 16)
        def _(r):
            at = pl.ds(pl.multiple_of(r * 16, 16), 16)
            total = self.total_s[at, pl.ds(0, item.columns)]
            for i, (condition, _) in enumerate(gots):
                total = total + jnp.where(condition, self.got_s[i, at, pl.ds(0, item.columns)].astype(F32), 0.0)
            put(at, total)

    def arrived(self, item, t, position):
        found, last_found = [], []
        for u in range(t):
            stage = item.stages[u]
            spot = position
            scale = 1
            for s in item.stages[t:]:
                scale *= s.size
            lead = 0
            for s in item.stages[u + 1 : t]:
                lead = lead * s.size + s.digit
            rows = pl.ds((lead * scale + spot) * item.width, item.width)
            last = stage.size - 2
            if stage.size == 2:
                back = jnp.where(stage.digit == 0, 1, 0)
                (last_found if u == t - 1 else found).append((stage.digit >= 0, item.recv[u].at[back, last, rows]))
            else:
                (last_found if u == t - 1 else found).append((stage.digit >= 1, item.recv[u].at[0, last, rows]))
                (last_found if u == t - 1 else found).append((stage.digit <= stage.size - 2, item.recv[u].at[1, last, rows]))
        return found, last_found

    def own_base(self, item, t):
        base = 0
        for s in item.stages[:t]:
            base = base + s.digit * s.stride
        return base

    def wait_last(self, item, t):
        if t < item.ready:
            return
        stage = item.stages[t]
        for back in range(2):
            me = stage.digit if back == 0 else stage.size - 1 - stage.digit

            @pl.when(me >= 1)
            def _(back=back):
                item.message(t, back, stage.size - 1, 0).wait_recv()

    def round(self, item, t, k):
        stage = item.stages[t]
        base = self.own_base(item, t)
        alone = t == 0 and k == 1
        if k == 1 and t > 0:
            self.wait_last(item, t - 1)

        @pl.loop(0, 2)
        def _(back):
            me = jnp.where(back == 0, stage.digit, stage.size - 1 - stage.digit)
            there = me + stage.size - k
            value = jnp.where(back == 0, there, stage.size - 1 - there)
            slot = jnp.where(value > stage.digit, value - 1, value)

            def rows_of(p):
                return pl.ds(pl.multiple_of(p * item.width, item.width), item.width)

            def gots_of(p):
                earlier = sum(self.arrived(item, t, value * stage.blocks + p), [])
                return earlier, [(me >= 1, item.recv[t].at[back, k - 2, rows_of(p)])] if k > 1 else []

            @pl.when(me <= k - 1)
            def _():
                if not alone:
                    self.start_gots(item, 0, gots_of(0)[0])

                def store(p, cols, total):
                    if alone:
                        item.send[t][slot, rows_of(p), cols] = total.astype(BF16)
                    else:
                        self.total_s[:, cols] = total

                def done(p):
                    if not alone:
                        if k > 1:

                            @pl.when((me >= 1) & (p == 0))
                            def _():
                                item.message(t, back, k - 1, 0).wait_recv()

                        def put(at, value):
                            rows = pl.ds(pl.multiple_of(p * item.width + at.start, 16), 16)
                            item.send[t][slot, rows, :] = value.astype(BF16)

                        earlier, own = gots_of(p)
                        self.start_gots(item, len(earlier), own)
                        self.add_gots(item, earlier + own, put)

                        @pl.when(p + 1 < stage.blocks)
                        def _():
                            self.start_gots(item, 0, gots_of(p + 1)[0])

                    item.message(t, back, k, slot, rows_of(p)).start()

                self.products(item, stage.blocks, lambda p: base + value * stage.stride + stage.offset(p), store, done)

    def out_copy(self, item):
        return pltpu.make_async_copy(self.out_s.at[:, pl.ds(0, item.columns)], item.out, self.out_sem)

    def finish(self, item):
        t = len(item.stages)
        self.wait_last(item, t - 1)
        gots = sum(self.arrived(item, t, 0), [])
        self.start_gots(item, 0, gots)

        def store(p, cols, total):
            self.total_s[:, cols] = total

        def put(at, value):
            self.out_s[at, pl.ds(0, item.columns)] = value

        self.settle()
        self.products(item, 1, lambda p: self.own_base(item, t), store, lambda p: self.add_gots(item, gots, put))
        self.out_copy(item).start()
        self.finished = item

    def settle(self):
        if self.finished is not None:
            self.out_copy(self.finished).wait()
        self.finished = None

    def drain(self, item, stages):
        for t in stages:
            for slot in range(item.stages[t].size - 1):
                item.message(t, 0, 1, slot).wait_send()


def stage_shapes(n, last_first, width, columns):
    sizes = digit_sizes(n)
    if last_first:
        sizes = sizes[1:] + sizes[:1]
    left, found = n, []
    for t, m in enumerate(sizes):
        left //= m
        found.append(
            (
                jax.ShapeDtypeStruct((2, m - 1, left * width, columns), BF16),
                pltpu.VMEM((m - 1, left * width, columns), BF16),
                pltpu.SemaphoreType.DMA((m - 1,)),
                pltpu.SemaphoreType.DMA((2, m - 1)),
            )
        )
    return found


def dot_tn(left, right):
    return lax.dot_general(left, right, (((0,), (0,)), ((), ())), preferred_element_type=F32)


class Reader:
    def __init__(self, refs):
        self.refs, self.at = refs, 0

    def __call__(self, count=None):
        start = self.at
        self.at += 1 if count is None else count
        return self.refs[start] if count is None else list(self.refs[start : self.at])


def column_blocks(left, n):
    tokens, features = left.shape
    width = features // n
    return left.reshape(tokens, n, width).transpose(1, 0, 2) if width % LANES else left


class TensorLine:
    def __init__(self):
        self.index = lax.axis_index("tensor")
        self.mate, self.peer, self.cross = self.index ^ 1, self.index ^ 2, self.index ^ 3


def copy_in(source, target, sem):
    copy = pltpu.make_async_copy(source, target, sem)
    copy.start()
    return copy


def remote(source, target, send_sem, recv_sem, axis, index):
    return pltpu.make_async_remote_copy(
        src_ref=source, dst_ref=target, send_sem=send_sem, recv_sem=recv_sem,
        device_id={axis: index}, device_id_type=pl.DeviceIdType.MESH,
    )


class TensorReduce:
    def __init__(self, line, part, from_mate, from_peer, own_v, got_v, send_v, send_sem, recv_sem, sem):
        self.line, self.part, self.from_mate, self.from_peer = line, part, from_mate, from_peer
        self.own_v, self.got_v, self.send_v, self.sem = own_v, got_v, send_v, sem
        self.rows = part.shape[0] // 4
        self.mates = [
            remote(self.block(line.cross), from_mate.at[0], send_sem.at[0], recv_sem.at[0], "tensor", line.mate),
            remote(self.block(line.mate), from_mate.at[1], send_sem.at[1], recv_sem.at[1], "tensor", line.mate),
        ]
        self.over = remote(send_v, from_peer, send_sem.at[2], recv_sem.at[2], "tensor", line.peer)

    def block(self, index):
        return self.part.at[pl.ds(pl.multiple_of(index * self.rows, self.rows), self.rows)]

    def start(self):
        for copy in self.mates:
            copy.start()

    def own_rows(self, index, at):
        if self.own_v is not None:
            return self.own_v[at, :].astype(F32)
        return self.part[pl.ds(pl.multiple_of(index * self.rows + at.start, 16), 16), :].astype(F32)

    def fetch_own(self, index):
        return [] if self.own_v is None else [copy_in(self.block(index), self.own_v, self.sem.at[0])]

    def middle(self):
        copies = self.fetch_own(self.line.peer)
        self.mates[0].wait_recv()
        copies.append(copy_in(self.from_mate.at[0], self.got_v.at[0], self.sem.at[1]))
        for copy in copies:
            copy.wait()

        @pl.loop(0, self.rows // 16)
        def _(r):
            at = pl.ds(pl.multiple_of(r * 16, 16), 16)
            self.send_v[at, :] = (self.own_rows(self.line.peer, at) + self.got_v[0, at, :].astype(F32)).astype(BF16)

        self.over.start()

    def end(self, use):
        copies = self.fetch_own(self.line.index)
        self.mates[1].wait_recv()
        copies.append(copy_in(self.from_mate.at[1], self.got_v.at[0], self.sem.at[1]))
        self.over.wait_recv()
        copies.append(copy_in(self.from_peer, self.got_v.at[1], self.sem.at[2]))
        for copy in copies:
            copy.wait()

        @pl.loop(0, self.rows // 16)
        def _(r):
            at = pl.ds(pl.multiple_of(r * 16, 16), 16)
            use(at, self.own_rows(self.line.index, at) + self.got_v[0, at, :].astype(F32) + self.got_v[1, at, :].astype(F32))

    def drain(self):
        for copy in self.mates:
            copy.wait_send()
        self.over.wait_send()

    @staticmethod
    def results(tokens, features):
        return [jax.ShapeDtypeStruct((2, tokens // 4, features), BF16), jax.ShapeDtypeStruct((tokens // 4, features), BF16)]

    @staticmethod
    def semaphores():
        return [pltpu.SemaphoreType.DMA((3,)), pltpu.SemaphoreType.DMA((3,)), pltpu.SemaphoreType.DMA((3,))]

    @staticmethod
    def buffers(tokens, features):
        rows = tokens // 4
        return [pltpu.VMEM((2, rows, features), BF16), pltpu.VMEM((rows, features), BF16)]


def norm_backward(values, gain, d_normed):
    inverse = lax.rsqrt(jnp.mean(values * values, axis=-1, keepdims=True) + epsilon)
    weighted = gain * d_normed
    inner = jnp.mean(weighted * values, axis=-1, keepdims=True)
    return inverse * weighted - values * (inverse * inverse * inverse * inner), d_normed * values * inverse


HBM = pl.BlockSpec(memory_space=pl.ANY)
IN_VMEM = pl.BlockSpec(memory_space=pltpu.VMEM)


class TensorGather:
    def __init__(self, line, own_v, out, send_sem, recv_sem):
        self.line, self.own_v, self.out, self.rows = line, own_v, out, own_v.shape[0]
        self.over = remote(own_v, self.block(line.index), send_sem.at[0], recv_sem.at[0], "tensor", line.peer)
        self.aside = remote(own_v, self.block(line.index), send_sem.at[1], recv_sem.at[1], "tensor", line.mate)
        self.onward = remote(self.block(line.peer), self.block(line.peer), send_sem.at[2], recv_sem.at[2], "tensor", line.mate)

    def block(self, index):
        return self.out.at[pl.ds(pl.multiple_of(index * self.rows, self.rows), self.rows)]

    def start(self):
        self.over.start()
        self.aside.start()

    def forward(self):
        self.over.wait_recv()
        self.onward.start()

    def drain(self):
        for copy in (self.over, self.aside, self.onward):
            copy.wait_send()

    @staticmethod
    def semaphores():
        return [pltpu.SemaphoreType.DMA((3,)), pltpu.SemaphoreType.DMA((3,))]


def main_kernel(n, width, units, *refs):
    take = Reader(refs)
    cot_own, w_first, w_branch, w_out, w_gate, w_up, w_down = take(7)
    stream, gain_one, gain, masks, vecs, w_cat = take(6)
    normed, cot, gated, branch, conv, states, product, middle, normed_two, from_mate_one, from_peer_one = take(11)
    d_middle, att, hidden_o, dgate_o, dup_o, dgated_o, dri_o, dbranch_o, part_out, dense_o, from_mate, from_peer = take(12)
    down_recv, (gate_recv, up_recv) = take(2), take(2)
    sums, gain_grad = take(2)
    (att_v,) = take(1)
    one_sems, cot_sems, two_sems, one_rs = take(2), take(2), take(2), take(3)
    one_sem, rs_send, rs_recv, rs_sem, ag_send, ag_recv, sem, engine_sem = take(8)
    item_sems = [take(2) for _ in range(4)]
    rows, features = stream.shape
    tokens, channels = conv.shape
    tile = 512
    line = TensorLine()
    twos = TensorGather(line, att_v, normed_two, *two_sems)
    two_v = att_v

    def forward_phase(
        wg_v, wb_v, wo_v, own_v, cot_v, block_v, gated_v, branch_v, conv_v, states_v, product_v,
        pre_s, a_s, b_s, part_v, rs_got, rs_send_v, middle_v,
    ):
        ones = TensorGather(line, own_v, normed, *one_sems)
        cots = TensorGather(line, cot_v, cot, *cot_sems)
        reduce = TensorReduce(line, part_v, from_mate_one, from_peer_one, None, rs_got, rs_send_v, *one_rs)
        loads = [copy_in(w_first, wg_v, one_sem.at[0]), copy_in(w_branch, wb_v, one_sem.at[1]), copy_in(w_out, wo_v, one_sem.at[2])]
        cot_load = copy_in(cot_own, cot_v, one_sem.at[3])

        def chunks(body):
            @pl.loop(0, rows // 16)
            def _(r):
                body(pl.ds(pl.multiple_of(r * 16, 16), 16))

        def norm(values, gains):
            inverse = lax.rsqrt(jnp.mean(values * values, axis=-1, keepdims=True) + epsilon)
            return (values * inverse * gains).astype(BF16)

        def first_norm(at):
            own_v[at, :] = norm(stream[at, :].astype(F32), gain_one[...])

        chunks(first_norm)
        ones.start()
        keep = [copy_in(own_v, ones.block(line.index), one_sem.at[4])]
        cot_load.wait()
        cots.start()
        keep.append(copy_in(cot_v, cots.block(line.index), one_sem.at[5]))

        def project(source, index):
            at = pl.ds(pl.multiple_of(index * rows, rows), rows)
            branch_v[at, :] = jnp.dot(source, wb_v[...], preferred_element_type=F32)
            gated_v[at, :] = jnp.dot(source, wg_v[...], preferred_element_type=F32)

        loads[0].wait()
        loads[1].wait()

        @pl.loop(0, 4)
        def _(b):
            index = line.index ^ b

            @pl.when(b == 0)
            def _():
                copy_in(own_v, block_v, one_sem.at[6]).wait()

            @pl.when(b == 1)
            def _():
                ones.aside.wait_recv()

            @pl.when(b == 2)
            def _():
                ones.forward()

            @pl.when(b == 3)
            def _():
                ones.onward.wait_recv()

            @pl.when(b > 0)
            def _():
                copy_in(ones.block(index), block_v, one_sem.at[6]).wait()

            project(block_v[...], index)

        outs = [copy_in(branch_v, branch, one_sem.at[7]), copy_in(gated_v, gated, one_sem.at[8])]
        mixer_forward_kernel(branch_v, gated_v, masks, vecs, w_cat, conv_v, states_v, product_v, pre_s, a_s, b_s)
        outs += [copy_in(conv_v, conv, one_sem.at[9]), copy_in(states_v, states, one_sem.at[10]), copy_in(product_v, product, one_sem.at[11])]
        loads[2].wait()

        def out_block(index):
            at = pl.ds(pl.multiple_of(index * rows, rows), rows)
            part_v[at, :] = jnp.dot(product_v[at, :], wo_v[...], preferred_element_type=F32).astype(BF16)

        @pl.loop(0, 4)
        def _(q):
            out_block(line.cross ^ q)

            @pl.when(q == 0)
            def _():
                reduce.mates[0].start()

            @pl.when(q == 1)
            def _():
                reduce.middle()

            @pl.when(q == 2)
            def _():
                reduce.mates[1].start()

        cots.forward()

        def second_norm(at, total):
            values = stream[at, :].astype(F32) + total
            middle_v[at, :] = values
            two_v[at, :] = norm(values, gain[...])

        reduce.end(second_norm)
        twos.start()
        keep += [copy_in(two_v, twos.block(line.index), one_sem.at[12]), copy_in(middle_v, middle, one_sem.at[13])]
        cots.aside.wait_recv()
        cots.onward.wait_recv()
        for copy in keep + outs:
            copy.wait()
        for gathered in (ones, cots):
            gathered.drain()
        reduce.drain()

    block = pltpu.VMEM((rows, features), BF16)
    wide = pltpu.VMEM((tokens, channels), F32)
    narrow = pltpu.VMEM((tokens, channels), BF16)
    lanes = pltpu.VMEM((channels // LANES, tokens, LANES), F32)
    pl.run_scoped(
        forward_phase,
        pltpu.VMEM(w_first.shape, BF16), pltpu.VMEM(w_branch.shape, BF16), pltpu.VMEM(w_out.shape, BF16),
        block, block, block,
        wide, wide, narrow, wide, narrow,
        pltpu.VMEM((tokens, 2 * channels), F32), lanes, lanes,
        pltpu.VMEM((tokens, features), BF16), *TensorReduce.buffers(tokens, features),
        pltpu.VMEM((rows, features), F32),
    )

    def backward_phase(hidden, *held):
        down_one, down_two, gate_send, up_send, left_s, got_s, total_s = held
        halves = [(down_one, *item_sems[0]), (down_two, *item_sems[1])]
        (gate_ss, gate_rs), (up_ss, up_rs) = item_sems[2:]
        engine = Engine(left_s, got_s, total_s, engine_sem)
        downs = [
            Item(
                make_stages(n, True), cot, hidden.at[:, pl.ds(q * (units // 2), units // 2)], width, 0,
                (None, [down_recv[q]], [send], [send_sem], [recv_sem]),
            )
            for q, (send, send_sem, recv_sem) in enumerate(halves)
        ]
        gather = TensorGather(line, att_v, att, ag_send, ag_recv)

        def rounds(item):
            return list(range(1, item.stages[0].size))

        def row_block(ref, index):
            return ref.at[pl.ds(pl.multiple_of(index * rows, rows), rows)]

        first, between, last = rounds(downs[0])[:1], rounds(downs[0])[1:-1], rounds(downs[0])[1:][-1:]
        gate = Item(make_stages(n, False), normed_two, hidden, width, 0, (None, [gate_recv], [gate_send], [gate_ss], [gate_rs]))
        half = hidden.at[:, pl.ds(0, units // 2)]
        up = Item(make_stages(n, False), normed_two, half, width, 0, (None, [up_recv], [up_send], [up_ss], [up_rs]))

        def take_rounds(item, numbers):
            for k in numbers:
                engine.round(item, 0, k)

        def tensor_phase(wg_v, wu_v, wd_v, dgate, dup, x_v, c_v, part, got_v, send_v, dmid_v, cot_v):
            gate.right, up.right = dgate, dup.at[:, pl.ds(0, units // 2)]
            weights = [copy_in(w_gate, wg_v, sem.at[0]), copy_in(w_up, wu_v, sem.at[1]), copy_in(w_down, wd_v, sem.at[2])]
            loads = [copy_in(middle, dmid_v, sem.at[3]), copy_in(row_block(cot, line.index), cot_v, sem.at[4])]
            copy_in(row_block(normed_two, line.index), x_v, sem.at[5])
            copy_in(row_block(cot, line.index), c_v, sem.at[6])
            for load in weights:
                load.wait()

            @pl.loop(0, 4)
            def _(b):
                index = line.index ^ b
                at = pl.ds(pl.multiple_of(index * rows, rows), rows)
                pltpu.make_async_copy(row_block(normed_two, index), x_v, sem.at[5]).wait()
                pltpu.make_async_copy(row_block(cot, index), c_v, sem.at[6]).wait()

                @pl.loop(0, units // tile)
                def _(j):
                    cols = pl.ds(pl.multiple_of(j * tile, tile), tile)
                    gate_pre = jnp.dot(x_v[...], wg_v[:, cols], preferred_element_type=F32)
                    up_pre = jnp.dot(x_v[...], wu_v[:, cols], preferred_element_type=F32)
                    d_hidden = dot_nt(c_v[...], wd_v[cols, :])
                    act, slope = gelu_parts(gate_pre)
                    hidden[at, cols] = (act * up_pre).astype(BF16)
                    dgate[at, cols] = (d_hidden * up_pre * slope).astype(BF16)
                    dup[at, cols] = (d_hidden * act).astype(BF16)

                @pl.when(b == 0)
                def _():
                    twos.aside.wait_recv()

                @pl.when(b == 1)
                def _():
                    twos.forward()

                @pl.when(b == 2)
                def _():
                    twos.onward.wait_recv()

                @pl.when(b < 3)
                def _():
                    following = line.index ^ (b + 1)
                    copy_in(row_block(normed_two, following), x_v, sem.at[5])
                    copy_in(row_block(cot, following), c_v, sem.at[6])

            twos.drain()
            outs = [copy_in(hidden, hidden_o, sem.at[0]), copy_in(dgate, dgate_o, sem.at[1]), copy_in(dup, dup_o, sem.at[2])]
            for item in downs:
                take_rounds(item, first)
            take_rounds(gate, rounds(gate))

            def stage(index, value):
                @pl.loop(0, features // tile)
                def _(j):
                    at, cols = pl.ds(pl.multiple_of(index * rows, rows), rows), pl.ds(pl.multiple_of(j * tile, tile), tile)
                    part[at, cols] = value(at, cols).astype(BF16)

            def two(at, cols):
                return dot_nt(dgate[at, :], wg_v[cols, :]) + dot_nt(dup[at, :], wu_v[cols, :])

            def out(at, cols):
                return jnp.dot(hidden[at, :], wd_v[:, cols], preferred_element_type=F32)

            reduce = TensorReduce(line, part, from_mate, from_peer, None, got_v, send_v, rs_send, rs_recv, rs_sem)
            @pl.loop(0, 4)
            def _(q):
                stage(line.cross ^ q, two)

                @pl.when(q == 0)
                def _():
                    reduce.mates[0].start()

                @pl.when(q == 1)
                def _():
                    reduce.middle()

                @pl.when(q == 2)
                def _():
                    reduce.mates[1].start()

            for item in downs:
                take_rounds(item, between)
            for load in loads:
                load.wait()
            gain_grad[...] = jnp.zeros_like(gain_grad)

            def use(at, total):
                back, terms = norm_backward(dmid_v[at, :], gain[...], total)
                value = cot_v[at, :].astype(F32) + back
                dmid_v[at, :] = value
                att_v[at, :] = value.astype(BF16)
                gain_grad[...] += fold_rows(terms)

            reduce.end(use)
            gather.start()
            keep = [copy_in(att_v, gather.block(line.index), sem.at[3]), copy_in(dmid_v, d_middle, sem.at[4])]
            take_rounds(up, rounds(up))
            reduce.drain()

            @pl.loop(0, 4)
            def _(b):
                stage(b, out)
                copy_in(row_block(part, b), row_block(part_out, b), sem.at[7])

            take_rounds(downs[0], last)
            gather.forward()
            for copy in outs + keep:
                copy.wait()
            pltpu.make_async_copy(part, part_out, sem.at[7]).wait()

        weight = pltpu.VMEM((features, units), BF16)
        block = pltpu.VMEM((rows, features), BF16)
        pl.run_scoped(
            tensor_phase,
            weight, weight, pltpu.VMEM((units, features), BF16),
            pltpu.VMEM((tokens, units), BF16), pltpu.VMEM((tokens, units), BF16),
            block, block, pltpu.VMEM((tokens, features), BF16),
            *TensorReduce.buffers(tokens, features),
            pltpu.VMEM((rows, features), F32), block,
        )

        def mixer_phase(gated_v, states_v, conv_v, dgated_v, dri_v, dbranch_v, block_v, w_v, dense_v, *scratch):
            loads = [copy_in(conv, conv_v, sem.at[1]), copy_in(w_out, w_v, sem.at[0])]
            loads += [copy_in(gated, gated_v, sem.at[2]), copy_in(states, states_v, sem.at[3])]
            mixer = MixerBackward(masks, vecs, w_cat, states_v, gated_v, conv_v, dgated_v, dri_v, dbranch_v, sums, *scratch)
            loads[0].wait()
            mixer.gates()
            take_rounds(downs[1], last)
            loads[1].wait()

            def product_gradient(index, source):
                mixer.a_s[pl.ds(pl.multiple_of(index * rows, rows), rows), :] = dot_nt(source[...], w_v[...])

            def block_copy(b):
                slot = lax.rem(b, 2)
                return pltpu.make_async_copy(row_block(att, line.index ^ b), block_v.at[slot], sem.at[4 + slot])

            block_copy(0).start()

            @pl.loop(0, 4)
            def _(b):
                @pl.when(b == 0)
                def _():
                    gather.aside.wait_recv()

                @pl.when(b == 2)
                def _():
                    gather.onward.wait_recv()

                @pl.when(b < 3)
                def _():
                    block_copy(b + 1).start()

                block_copy(b).wait()
                product_gradient(line.index ^ b, block_v.at[lax.rem(b, 2)])

            loads[2].wait()
            loads[3].wait()
            mixer.factors(gated_v)
            again = copy_in(branch, gated_v, sem.at[2])
            outs = [copy_in(dgated_v, dgated_o, sem.at[1])]
            mixer.scan()
            mixer.gate_gradients()
            outs.append(copy_in(dri_v, dri_o, sem.at[3]))
            again.wait()
            mixer.convolution()
            outs.append(copy_in(dbranch_v, dbranch_o, sem.at[0]))

            @pl.loop(0, 2 * channels // 256)
            def _(j):
                cols = pl.ds(pl.multiple_of(j * 256, 256), 256)
                dense_v[:, cols] = dot_tn(conv_v[...], dri_v[:, cols])

            outs.append(copy_in(dense_v, dense_o, sem.at[4]))
            for copy in outs:
                copy.wait()

        pl.run_scoped(
            mixer_phase,
            pltpu.VMEM((tokens, channels), F32),
            pltpu.VMEM((tokens, channels), F32),
            pltpu.VMEM((tokens, channels), BF16),
            pltpu.VMEM((tokens, channels), BF16),
            pltpu.VMEM((tokens, 2 * channels), BF16),
            pltpu.VMEM((tokens, channels), BF16),
            pltpu.VMEM((2, rows, features), BF16),
            pltpu.VMEM((channels, features), BF16),
            pltpu.VMEM((channels, 2 * channels), F32),
            *MixerBackward.scratch(tokens, channels),
        )
        gather.drain()
        for item in (*downs, gate, up):
            engine.drain(item, [0])
            engine.wait_last(item, 0)

    down = stage_shapes(n, True, width, units // 2)[0][1]
    gate = stage_shapes(n, False, width, units)[0][1]
    up = stage_shapes(n, False, width, units // 2)[0][1]
    pl.run_scoped(
        backward_phase,
        pltpu.VMEM((tokens, units), BF16), down, down, gate, up,
        pltpu.VMEM((2, tokens, max(width, LANES)), BF16),
        pltpu.VMEM((2, width, units), BF16),
        pltpu.VMEM((width, units), F32),
    )


def main_part(cot_own, w_first, w_branch, w_out, w_gate, w_up, w_down, stream, gain_one, gain_two, masks, vecs, w_cat):
    n = lax.axis_size("dp")
    rows, features = stream.shape
    tokens, channels, units, width = 4 * rows, w_first.shape[1], w_gate.shape[1], features // n
    down = stage_shapes(n, True, width, units // 2)[0]
    gate = stage_shapes(n, False, width, units)[0]
    up = stage_shapes(n, False, width, units // 2)[0]
    dma = pltpu.SemaphoreType.DMA
    whole = jax.ShapeDtypeStruct((tokens, features), BF16)
    part = jax.ShapeDtypeStruct((rows, features), F32)
    hide = jax.ShapeDtypeStruct((tokens, units), BF16)
    wide = jax.ShapeDtypeStruct((tokens, channels), F32)
    narrow = jax.ShapeDtypeStruct((tokens, channels), BF16)
    sums = TensorReduce.results(tokens, features)
    results = [whole, whole, wide, wide, narrow, wide, narrow, part, whole, *sums]
    results += [part, whole, hide, hide, hide, narrow, jax.ShapeDtypeStruct((tokens, 2 * channels), BF16), narrow, whole]
    results += [jax.ShapeDtypeStruct((channels, 2 * channels), F32), *sums]
    results += [down[0], down[0], gate[0], up[0]]
    gathers = TensorGather.semaphores()
    return pl.pallas_call(
        functools.partial(main_kernel, n, width, units),
        out_shape=[*results, jax.ShapeDtypeStruct((8, 8, channels), F32), jax.ShapeDtypeStruct((8, features), F32)],
        in_specs=[HBM] * 7 + [IN_VMEM] * 6,
        out_specs=[HBM] * len(results) + [IN_VMEM] * 2,
        scratch_shapes=[
            pltpu.VMEM((rows, features), BF16),
            *gathers, *gathers, *gathers, *TensorReduce.semaphores(), dma((14,)),
            *TensorReduce.semaphores(), *gathers, dma((8,)), dma((4,)),
            *down[2:4], *down[2:4], *gate[2:4], *up[2:4],
        ],
        compiler_params=pltpu.CompilerParams(vmem_limit_bytes=VMEM_BYTES, has_side_effects=True),
        cost_estimate=pl.CostEstimate(flops=60 * 10**9, bytes_accessed=120 * 10**6, transcendentals=14 * tokens * channels),
        name="main_part",
    )(cot_own, w_first, w_branch, w_out, w_gate, w_up, w_down, stream, gain_one, gain_two, masks, vecs, w_cat)


def gather_sums(gains, sends, recvs, send_sems, recv_sems):
    n, line = lax.axis_size("dp"), TensorLine()
    hops = [("tensor", line.mate), ("tensor", line.peer)]
    bit = 1
    while bit < n:
        hops.append(("dp", lax.axis_index("dp") ^ bit))
        bit *= 2
    copies = [remote(sends.at[s], recvs.at[s], send_sems.at[s], recv_sems.at[s], *hop) for s, hop in enumerate(hops)]

    def begin(s):
        sends[s] = gains[...] if s == 0 else sends[s - 1] + recvs[s - 1]
        copies[s].start()

    def step(s):
        if s > 0:
            copies[s - 1].wait_recv()
        if s < len(copies):
            begin(s)
        else:
            gains[...] = sends[s - 1] + recvs[s - 1]
            for copy in copies:
                copy.wait_send()

    return [functools.partial(step, s) for s in range(len(copies) + 1)]


def finish_kernel(n, width, plan, order, lefts_of, keep, readies, columns, out_of, *refs):
    take = Reader(refs)
    count, n_outs = len(plan), max(o for o, _ in out_of) + 1
    part_out, middle, d_middle, stream, w_gate, w_branch = take(6)
    gain, gain_grad_two = take(2)
    lefts, rights_hbm = take(max(lefts_of) + 1), take(n_outs)
    shapes = [stage_shapes(n, plan[i], width, columns[i]) for i in range(count)]
    given = [take(readies[i]) for i in range(count)]
    stream_grad_o, stream_out_o = take(2)
    outs = take(n_outs)
    (part,) = take(1)
    reduces = [take(2), take(2)]
    recv = [given[i] + take(len(shapes[i]) - readies[i]) for i in range(count)]
    (gains,) = take(1)
    rights = take(n_outs)
    wg_v, wb_v, stage_v = take(3)
    nones = [[None] * r for r in readies]
    sends = [nones[i] + take(len(shapes[i]) - readies[i]) for i in range(count)]
    send_sems = [nones[i] + take(len(shapes[i]) - readies[i]) for i in range(count)]
    recv_sems = [nones[i] + take(len(shapes[i]) - readies[i]) for i in range(count)]
    left_vs = take(max(lefts_of) + 1)
    left_s, got_s, total_s, out_s, own_v, got_v, send_v, send_w = take(8)
    value_v, base_v, gain_sends, gain_recvs = take(4)
    rs_sems = [take(3), take(3)]
    gain_ss, gain_rs, right_sem, sem, engine_sem, out_sem = take(6)

    line = TensorLine()
    engine = Engine(left_s, got_s, total_s, engine_sem, out_s, out_sem)
    tensor = [
        TensorReduce(line, source, *reduces[q], own_v, got_v, (send_v, send_w)[q], *rs_sems[q])
        for q, source in enumerate((part, part_out))
    ]
    tensor[1].start()
    loads, weights, left_loads = {}, [], {}

    def issue(kind, i):
        if kind == "left" and i in keep and i not in left_loads:
            left_loads[i] = copy_in(lefts[i], left_vs[i], right_sem.at[n_outs + 2 + i])
        if kind == "right" and i not in loads:
            loads[i] = copy_in(rights_hbm[i], rights[i], right_sem.at[i])

    def issue_for(i):
        if i >= 0:
            issue("right", out_of[i][0])
            issue("left", lefts_of[i])
        elif not weights:
            issue("right", n_outs - 2)
            issue("right", n_outs - 1)
            weights.extend([copy_in(w_gate, wg_v, right_sem.at[n_outs]), copy_in(w_branch, wb_v, right_sem.at[n_outs + 1])])

    loaded = set()

    def load_left(i):
        if left_loads.get(i) is not None:
            left_loads[i].wait()
            left_loads[i] = None

    def load(i):
        if i not in loaded:
            loads[i].wait()
            loaded.add(i)

    def columns_of(i):
        return pl.ds(out_of[i][1], columns[i])

    items = [
        Item(
            make_stages(n, plan[i]), lefts[lefts_of[i]], rights[out_of[i][0]].at[:, columns_of(i)], width, readies[i],
            (outs[out_of[i][0]].at[:, columns_of(i)], recv[i], sends[i], send_sems[i], recv_sems[i]),
            left_vs[lefts_of[i]] if lefts_of[i] in keep else None,
        )
        for i in range(count)
    ]

    rows, features = stream.shape

    def stage(index):
        at = pl.ds(pl.multiple_of(index * rows, rows), rows)

        @pl.loop(0, features // 512)
        def _(j):
            cols = pl.ds(pl.multiple_of(j * 512, 512), 512)
            total = dot_nt(rights[n_outs - 2][at, :], wg_v[cols, :]) + dot_nt(rights[n_outs - 1][at, :], wb_v[cols, :])
            stage_v[:, cols] = total.astype(BF16)

        copy_in(stage_v, tensor[0].block(index), sem.at[0]).wait()

    def stage_pair(first, mate):
        @pl.loop(0, 2)
        def _(q):
            stage(first ^ q)

            @pl.when(q == 0)
            def _():
                tensor[0].mates[mate].start()

    def part_first():
        for i in (n_outs - 2, n_outs - 1):
            load(i)
        for copy in weights:
            copy.wait()
        stage_pair(line.cross, 0)

    def part_second():
        stage_pair(line.mate, 1)

    def grad_end():
        copies = [copy_in(stream, value_v, sem.at[0]), copy_in(d_middle, base_v, sem.at[1])]
        for copy in copies:
            copy.wait()
        gains[...] = jnp.zeros_like(gains)

        def use(at, total):
            back, terms = norm_backward(value_v[at, :].astype(F32), gain[...], total)
            base_v[at, :] = base_v[at, :] + back
            gains[...] += fold_rows(terms)

        tensor[0].end(use)
        copy_in(base_v, stream_grad_o, sem.at[0]).wait()
        first = jnp.sum(gains[...], axis=0, keepdims=True)
        second = jnp.sum(gain_grad_two[...], axis=0, keepdims=True)
        pick = lax.broadcasted_iota(jnp.int32, gains.shape, 0)
        gains[...] = jnp.where(pick == 0, first, jnp.where(pick == 1, second, 0.0))

    def out_end():
        copy_in(middle, base_v, sem.at[0]).wait()

        def use(at, total):
            base_v[at, :] = base_v[at, :] + total

        tensor[1].end(use)
        copy_in(base_v, stream_out_o, sem.at[0]).wait()

    extra = [part_first, tensor[0].middle, part_second, tensor[1].middle, grad_end, out_end]
    extra += gather_sums(gains, gain_sends, gain_recvs, gain_ss, gain_rs)
    for at, (i, t, k) in enumerate(order):
        for ahead in order[at : at + 3]:
            issue_for(ahead[0])
        if i < 0:
            if extra:
                extra.pop(0)()
            continue
        load(out_of[i][0])
        load_left(lefts_of[i])
        if t < len(shapes[i]):
            engine.round(items[i], t, k)
        else:
            engine.finish(items[i])
    for step in extra:
        step()
    engine.settle()
    for i, item in enumerate(items):
        engine.drain(item, range(readies[i], len(shapes[i])))
    for reduce in tensor:
        reduce.drain()


def task_order(plan, readies, names, n):
    tasks = []
    for last_first, ready in zip(plan, readies):
        sizes = digit_sizes(n)
        if last_first:
            sizes = sizes[1:] + sizes[:1]
        i = len(tasks)
        tasks.append([(i, t, k) for t, m in enumerate(sizes) for k in range(1, m) if t >= ready] + [(i, len(sizes), 0)])
    out, at = [], [0] * len(plan)
    for i in names:
        if i < 0:
            out.append((-1, 0, 0))
        elif at[i] < len(tasks[i]):
            out.append(tasks[i][at[i]])
            at[i] += 1
    for i in range(len(plan)):
        out += tasks[i][at[i] :]
    return out


def finish(part_out, middle, d_middle, stream, w_gate, w_branch, gain, gain_grad_two, lefts, lefts_of, rights, given, plan, out_of, names, keep):
    n = lax.axis_size("dp")
    tokens, features = part_out.shape
    width, rows = features // n, tokens // 4
    readies = [len(g) for g in given]
    pieces = [sum(o == q for o, _ in out_of) for q in range(len(rights))]
    columns = [rights[o].shape[1] // pieces[o] for o, _ in out_of]
    out_of = [(o, q * c) for (o, q), c in zip(out_of, columns)]
    widest = max(columns)
    keep = () if width % LANES else keep
    shapes = [stage_shapes(n, last_first, width, c)[ready:] for last_first, c, ready in zip(plan, columns, readies)]
    steps = 2 + (n - 1).bit_length()
    dma = pltpu.SemaphoreType.DMA
    stream_shape = jax.ShapeDtypeStruct((rows, features), F32)
    out_shape = [stream_shape, stream_shape] + [jax.ShapeDtypeStruct((width, r.shape[1]), F32) for r in rights]
    out_shape += [jax.ShapeDtypeStruct((tokens, features), BF16)]
    out_shape += TensorReduce.results(tokens, features) * 2 + [s[0] for item in shapes for s in item]
    results = pl.pallas_call(
        functools.partial(finish_kernel, n, width, plan, task_order(plan, readies, names, n), lefts_of, keep, readies, columns, out_of),
        out_shape=[*out_shape, jax.ShapeDtypeStruct((8, features), F32)],
        in_specs=[HBM] * 6 + [IN_VMEM] * 2 + [HBM] * (len(lefts) + len(rights) + sum(readies)),
        out_specs=[HBM] * len(out_shape) + [IN_VMEM],
        scratch_shapes=[
            *[pltpu.VMEM(r.shape, BF16) for r in rights],
            pltpu.VMEM(w_gate.shape, BF16), pltpu.VMEM(w_branch.shape, BF16), pltpu.VMEM((rows, features), BF16),
            *[s[1] for item in shapes for s in item],
            *[s[2] for item in shapes for s in item],
            *[s[3] for item in shapes for s in item],
            *[pltpu.VMEM((tokens, features) if i in keep else (8, features), BF16) for i in range(len(lefts))],
            pltpu.VMEM((2, tokens, width), BF16),
            pltpu.VMEM((2 * len(digit_sizes(n)), width, widest), BF16),
            pltpu.VMEM((width, widest), F32), pltpu.VMEM((width, widest), F32),
            pltpu.VMEM((rows, features), BF16), *TensorReduce.buffers(tokens, features),
            pltpu.VMEM((rows, features), BF16),
            pltpu.VMEM((rows, features), BF16),
            pltpu.VMEM((rows, features), F32),
            pltpu.VMEM((steps, 8, features), F32),
            pltpu.VMEM((steps, 8, features), F32),
            *TensorReduce.semaphores(),
            *TensorReduce.semaphores(),
            dma((steps,)), dma((steps,)), dma((len(rights) + 2 + len(lefts),)), dma((2,)), dma((2 + 2 * len(digit_sizes(n)),)), dma,
        ],
        compiler_params=pltpu.CompilerParams(vmem_limit_bytes=VMEM_BYTES, has_side_effects=True),
        cost_estimate=pl.CostEstimate(
            flops=2 * tokens * features * sum(columns), bytes_accessed=4 * features * sum(columns), transcendentals=0
        ),
        name="finish",
    )(
        part_out, middle, d_middle, stream, w_gate, w_branch, gain, gain_grad_two,
        *[column_blocks(v, n) for v in lefts], *rights, *[g for item in given for g in item],
    )
    return results[0], results[1], results[2 : 2 + len(rights)], results[-1]

DP_PLAN = [True, True, False, False, False, False, False, False]
DP_OUTS = [(0, 0), (0, 1), (1, 0), (2, 0), (2, 1), (3, 0), (4, 0), (5, 0)]
DP_ORDER = [2, 5, 3, -1, 7, 2, 4, -1, 5, -1, -1, 3, 2, -1, 7, 6, 5, -1, -1, 3, 5, -1, 4, 2, -1, 1, 7, 5, -1, 4, 6, -1, 0, 7, 1, 6, 4, -1, 3, 0, 6, 7, 4, 6]


def spread_heads(*weights):
    heads, width = weights[0].shape[:2]
    total = len(weights) * heads * width
    rows = []
    for h in range(heads):
        row = 0
        for q, weight in enumerate(weights):
            before = (q * heads + h) * width
            row = row + jnp.pad(weight[h], ((0, 0), (before, total - before - width)))
        rows.append(row)
    return jnp.concatenate(rows)


def on_device(
    stream_in, segments, first_gain, gelu_gate_weight, recurrent_branch_weight, conv_kernel, conv_bias, recur_weight, recur_bias,
    inlet_weight, inlet_bias, decay_param, recurrent_output_weight, second_gain, gate_projection_weight, up_projection_weight,
    down_projection_weight, cotangent,
):
    seq_len = segments.shape[1]
    heads, head_width = recur_weight.shape[:2]
    ids = jnp.pad(segments[0], (3, 8), constant_values=-1)
    same = [(ids[3 - k : 3 - k + seq_len] == segments[0]).astype(F32) for k in range(1, 4)]
    masks = jnp.pad(jnp.stack(same, axis=1), ((0, 8), (0, 5)))
    softplus = jax.nn.softplus(-decay_param)
    vecs = jnp.concatenate([conv_kernel, jnp.stack([conv_bias, recur_bias, inlet_bias, softplus])])
    w_cat = spread_heads(recur_weight, inlet_weight)

    (
        normed, cot, _, _, _, _, product, middle, normed_two, _, _,
        d_middle, d_attended, hidden, d_gate, d_up, d_gated, _, d_branch, part_out, dense, _, _, *gots, sums, gain_two,
    ) = main_part(
        cotangent[0], gelu_gate_weight, recurrent_branch_weight, recurrent_output_weight, gate_projection_weight,
        up_projection_weight, down_projection_weight, stream_in[0], first_gain[None], second_gain[None], masks, vecs, w_cat,
    )
    stream_grad, stream_out, gradients, gains = finish(
        part_out, middle, d_middle, stream_in[0], gelu_gate_weight, recurrent_branch_weight, first_gain[None], gain_two,
        [cot, normed_two, d_attended, normed], [0, 0, 1, 1, 1, 2, 3, 3], [hidden, d_gate, d_up, product, d_gated, d_branch],
        [*([g] for g in gots), [], [], [], []], DP_PLAN, DP_OUTS, DP_ORDER, (1, 3),
    )
    down_gradient, gate_gradient, up_gradient, output_gradient, gated_gradient, branch_gradient = gradients

    width = heads * head_width
    blocks = [dense[h * head_width : (h + 1) * head_width, :] for h in range(heads)]
    rows = [blocks[h][:, q * width + h * head_width :][:, :head_width] for q in range(2) for h in range(heads)]
    sums = jnp.sum(sums, axis=1)
    rows += [sums[:, h * head_width : (h + 1) * head_width] for h in range(heads)]
    small = lax.psum(jnp.concatenate(rows).astype(BF16), "dp").astype(F32)
    grad_recur, grad_inlet = small[: 2 * width].reshape(2, heads, head_width, head_width)
    sums = jnp.concatenate([small[2 * width + 8 * h :][:8] for h in range(heads)], axis=1)
    grad_decay = decay_scale * jax.nn.sigmoid(-decay_param) * sums[7]
    return (
        stream_out[None], stream_grad[None], gains[0], gated_gradient, branch_gradient, sums[:4], sums[4], grad_recur, sums[5],
        grad_inlet, sums[6], grad_decay, output_gradient.T, gains[1], gate_gradient, up_gradient, down_gradient.T,
    )


def solution(mesh):
    in_specs = (
        P("dp", "tensor", None),
        P("dp", None),
        P(),
        P(None, "tensor"),
        P(None, "tensor"),
        P(None, "tensor"),
        P("tensor"),
        P("tensor", None, None),
        P("tensor"),
        P("tensor", None, None),
        P("tensor"),
        P("tensor"),
        P("tensor", None),
        P(),
        P(None, "tensor"),
        P(None, "tensor"),
        P("tensor", None),
        P("dp", "tensor", None),
    )
    out_specs = (
        P("dp", "tensor", None),
        P("dp", "tensor", None),
        P(),
        P("dp", "tensor"),
        P("dp", "tensor"),
        P(None, "tensor"),
        P("tensor"),
        P("tensor", None, None),
        P("tensor"),
        P("tensor", None, None),
        P("tensor"),
        P("tensor"),
        P("tensor", "dp"),
        P(),
        P("dp", "tensor"),
        P("dp", "tensor"),
        P("tensor", "dp"),
    )
    return jax.shard_map(
        on_device, mesh=mesh, in_specs=in_specs, out_specs=out_specs, check_vma=False
    )
```

profile of v0, /device:TPU:0, one launch (start us, length us, event | category | flops | bytes accessed | tf_op | source)
XLA Modules:
  0.0 483.3 jit_solution(12910631928053728017)
XLA Ops:
  7.2 1.0 slice_bitcast_fusion.7
  8.3 1.0 slice_bitcast_fusion.6
  9.3 0.9 fusion
  10.3 0.3 copy.42
  10.6 0.9 pad_convert_fusion.refs_10_
  11.4 0.7 compare_select_fusion
  12.1 0.7 stack.32
  12.8 0.7 stack.33
  13.5 0.7 stack.34
  14.2 0.2 pad_add_fusion
  14.6 1.3 pad_maximum_fusion.refs_12_
  15.8 0.6 concatenate.13.refs_11_
  16.5 241.6 %main_part.1 = (bf16[1024,2048]{1,0:T(8,128)(2,1)}, bf16[1024,2048]{1,0:T(8,128)(2,1)}, f32[1024,640]{1,0:T(8,128)}, f32[1024,640]{1,0:T(8,128)}, bf16[1024,640]...) custom-call(bf16[256,2048]{1,0:T(8,128)(2,1)} %bitcast.38, ...), custom_call_target="tpu_custom_call" | custom-call | flops 60000002048 | bytes 120000000 | tf_op jit(solution)/shard_map/main_part/pallas_call | solution.py:1069
  258.1 2.1 convert.34
  261.2 0.8 copy-done.4
  262.0 195.9 %finish.1 = (f32[256,2048]{1,0:T(8,128)}, f32[256,2048]{1,0:T(8,128)}, f32[256,1536]{1,0:T(8,128)}, f32[256,1536]{1,0:T(8,128)}, f32[256,1536]{1,0:T(8,128)}, /*...) custom-call(bf16[1024,2048]{1,0:T(8,128)(2,1)} %get-tuple-element.46, ...), custom_call_target="tpu_custom_call" | custom-call | flops 27380416512 | bytes 53477376 | tf_op jit(solution)/shard_map/finish/pallas_call | solution.py:1306
  458.0 3.1 copy.44
  461.1 1.1 copy.43
  462.2 1.5 fusion.5
  463.7 0.7 fusion.4
  464.4 0.7 maximum_reduce_fusion
  465.2 0.6 multiply_multiply_fusion
  465.8 0.6 slice.199
  466.4 2.2 fusion.3
  468.6 1.3 copy.63
  469.9 1.0 copy-done
  470.9 1.3 copy.64
  472.3 0.2 copy-done.6
  472.5 0.8 copy.65
  473.3 0.8 copy.66
  474.1 1.1 copy.67
  475.3 1.1 copy.68
  (42 shorter events, 1.2 us)
Async XLA Ops:
  7.2 456.5 %all-reduce.12.cloned.1.call-start = ((), (), s32[]{:S(2)}) async-start(), calls=%async_computation | async-start | bytes 1343488 | tf_op jit(solution)/shard_map/psum | solution.py:1393
  14.4 1.4 copy-start.10
  258.1 2.8 copy-start.8
  261.2 0.8 copy-start.4
  458.0 3.1 copy-start.7
  458.0 7.2 %copy-start.9 = (f32[640]{0:T(1024)S(1)}, f32[640]{0:T(1024)}, u32[]{:S(2)}) copy-start(f32[640]{0:T(1024)} %param.29) | copy-start | bytes 7684
  461.1 7.5 %copy-start.1 = (f32[256,2048]{1,0:T(8,128)S(1)}, f32[256,2048]{1,0:T(8,128)}, u32[]{:S(2)}) copy-start(f32[256,2048]{1,0:T(8,128)} %get-tuple-element.64) | copy-start | bytes 6291460
  468.6 2.3 copy-start
  470.9 1.5 copy-start.6
  470.9 2.4 copy-start.5
  470.9 3.2 copy-start.3
  473.3 2.0 copy-start.2
Sparse Core Ops, SparseCore 0:
  262.2 81.4 all-reduce.11
where the time goes:
time: 488 us; the launch traced here: 483 us
  Pallas kernels  438 us (90%)
  local copies, waits for them, and re-layouts  23.8 us (5%)
  between operations  14.3 us (3%)
  other arithmetic  7.65 us (2%)
    pallas_call x1, Pallas kernels, main_part(): pl.pallas_call(functools.partial(main_kernel, n, width, units), out_shape...  242 us
    pallas_call x1, Pallas kernels, finish(): pl.pallas_call(functools.partial(finish_kernel, n, width, plan, task_orde...  196 us
    unnamed x41, local copies, waits for them, and re-layouts  13.6 us
  transfers between devices with their start and end apart: 1, of which 0 were waited for; matrix products, arithmetic and copies ran while one was open for 1% of the time, Pallas kernels for 41%

commit v1 on v0

--- a/solution.py
+++ b/solution.py
@@ -887,9 +887,9 @@
 
             twos.drain()
             outs = [copy_in(hidden, hidden_o, sem.at[0]), copy_in(dgate, dgate_o, sem.at[1]), copy_in(dup, dup_o, sem.at[2])]
-            for item in downs:
-                take_rounds(item, first)
+            take_rounds(downs[0], first)
             take_rounds(gate, rounds(gate))
+            take_rounds(downs[1], first)
 
             def stage(index, value):
                 @pl.loop(0, features // tile)
@@ -1368,7 +1368,10 @@
     same = [(ids[3 - k : 3 - k + seq_len] == segments[0]).astype(F32) for k in range(1, 4)]
     masks = jnp.pad(jnp.stack(same, axis=1), ((0, 8), (0, 5)))
     softplus = jax.nn.softplus(-decay_param)
-    vecs = jnp.concatenate([conv_kernel, jnp.stack([conv_bias, recur_bias, inlet_bias, softplus])])
+    vecs = jnp.pad(conv_kernel, ((0, 4), (0, 0)))
+    row = lax.broadcasted_iota(jnp.int32, vecs.shape, 0)
+    for r, vec in enumerate((conv_bias, recur_bias, inlet_bias, softplus), conv_kernel.shape[0]):
+        vecs = jnp.where(row == r, vec[None], vecs)
     w_cat = spread_heads(recur_weight, inlet_weight)
 
     (

time: 488 us -> 486 us (level)
    unnamed x41 -> x47, local copies, waits for them, and re-layouts: 13.6 us -> 13.6 us
where the time goes in v1:
time: 486 us; the launch traced here: 481 us
  Pallas kernels  438 us (90%)
  local copies, waits for them, and re-layouts  21.1 us (4%)
  between operations  14.3 us (3%)
  other arithmetic  8.35 us (2%)
    pallas_call x1, Pallas kernels, main_part(): pl.pallas_call(functools.partial(main_kernel, n, width, units), out_shape...  239 us
    pallas_call x1, Pallas kernels, finish(): pl.pallas_call(functools.partial(finish_kernel, n, width, plan, task_orde...  198 us
    unnamed x47, local copies, waits for them, and re-layouts  13.6 us
  transfers between devices with their start and end apart: 1, of which 0 were waited for; matrix products, arithmetic and copies ran while one was open for 1% of the time, Pallas kernels for 41%

profile of v1, /device:TPU:0, one launch (start us, length us, event | category | flops | bytes accessed | tf_op | source)
XLA Modules:
  0.0 481.4 jit_solution(4784819929138733949)
XLA Ops:
  7.3 1.0 slice_bitcast_fusion.7
  8.3 1.0 slice_bitcast_fusion.6
  9.3 0.9 fusion
  10.3 0.3 copy.42
  10.6 0.9 pad_convert_fusion.refs_10_
  11.5 0.7 compare_select_fusion
  12.2 0.2 pad_add_fusion
  12.4 0.1 pad_add_fusion.2
  12.5 1.3 pad_maximum_fusion.refs_12_
  13.8 0.7 select_select_fusion.refs_11_
  14.5 239.3 %main_part.1 = (bf16[1024,2048]{1,0:T(8,128)(2,1)}, bf16[1024,2048]{1,0:T(8,128)(2,1)}, f32[1024,640]{1,0:T(8,128)}, f32[1024,640]{1,0:T(8,128)}, bf16[1024,640]...) custom-call(bf16[256,2048]{1,0:T(8,128)(2,1)} %bitcast.38, ...), custom_call_target="tpu_custom_call" | custom-call | flops 60000002048 | bytes 120000000 | tf_op jit(solution)/shard_map/main_part/pallas_call | solution.py:1069
  253.8 2.1 convert.34
  256.0 0.1 slice_dynamic-update-slice_fusion.6
  256.1 0.1 slice_dynamic-update-slice_fusion.5
  256.9 0.8 copy-done.4
  257.8 198.3 %finish.1 = (f32[256,2048]{1,0:T(8,128)}, f32[256,2048]{1,0:T(8,128)}, f32[256,1536]{1,0:T(8,128)}, f32[256,1536]{1,0:T(8,128)}, f32[256,1536]{1,0:T(8,128)}, /*...) custom-call(bf16[1024,2048]{1,0:T(8,128)(2,1)} %get-tuple-element.46, ...), custom_call_target="tpu_custom_call" | custom-call | flops 27380416512 | bytes 53477376 | tf_op jit(solution)/shard_map/finish/pallas_call | solution.py:1306
  456.1 3.1 copy.44
  459.2 1.1 copy.43
  460.2 1.5 fusion.5
  461.8 0.7 fusion.4
  462.5 0.7 maximum_reduce_fusion
  463.2 0.6 multiply_multiply_fusion
  463.9 0.6 slice.199
  464.5 2.2 fusion.3
  466.7 1.3 copy.63
  468.0 1.0 copy-done
  469.0 1.3 copy.64
  470.4 0.2 copy-done.6
  470.5 0.8 copy.65
  471.4 0.8 copy.66
  472.2 1.1 copy.67
  473.4 1.1 copy.68
  (46 shorter events, 0.9 us)
Async XLA Ops:
  7.2 454.6 %all-reduce.13.cloned.1.call-start = ((), (), s32[]{:S(2)}) async-start(), calls=%async_computation | async-start | bytes 1343488 | tf_op jit(solution)/shard_map/psum | solution.py:1396
  12.4 1.5 copy-start.10
  12.4 1.5 copy-start.11
  12.4 1.4 copy-start.12
  12.4 1.4 copy-start.13
  253.8 2.8 copy-start.8
  256.9 0.8 copy-start.4
  456.1 3.1 copy-start.7
  456.1 7.2 %copy-start.9 = (f32[640]{0:T(1024)S(1)}, f32[640]{0:T(1024)}, u32[]{:S(2)}) copy-start(f32[640]{0:T(1024)} %param.29) | copy-start | bytes 7684
  459.2 7.5 %copy-start.1 = (f32[256,2048]{1,0:T(8,128)S(1)}, f32[256,2048]{1,0:T(8,128)}, u32[]{:S(2)}) copy-start(f32[256,2048]{1,0:T(8,128)} %get-tuple-element.64) | copy-start | bytes 6291460
  466.7 2.3 copy-start
  469.0 1.5 copy-start.6
  469.0 2.4 copy-start.5
  469.0 3.2 copy-start.3
  471.4 2.0 copy-start.2
Sparse Core Ops, SparseCore 0:
  257.9 83.9 all-reduce.12
